TPU v7x, 32 devices: a whole 2x2x4 slice. The times are simulated.
32 devices in a mesh: gx: 2 (over x), gy: 4 (over z), gz: 4 (over y, core).
Axes of the slice: x: 2, y: 2, z: 4, core: 2. Of those that a mesh axis runs over, the one named last changes fastest.
Arguments:
- local_displacement: float32 [2, 4, 4, 6, 128, 128], P('gx', 'gy', 'gz'), may hold values from -6 to 6
- coarse_load: float32 [2, 4, 4, 6, 128], P('gx', 'gy', 'gz'), may hold values from -12 to 12
- flexibility: float32 [2, 4, 4, 768, 768], P('gx', 'gy', 'gz'), as said below
- block_map: int32 [2, 4, 4, 768], P('gx', 'gy', 'gz'), may hold values from 0 to 767, each once within a row
- mode_counts: int32 [2, 4, 4], P('gx', 'gy', 'gz'), may hold values from 3 to 6, as said below
- mode_traces: float32 [2, 4, 4, 6, 6, 128], P('gx', 'gy', 'gz')
- coarse_rows: float32 [2, 4, 4, 6, 192], P('gx', 'gy', 'gz'), as said below
- stored_dirs: float32 [2, 4, 4, 40, 6, 128], P('gx', 'gy', 'gz'), as said below
- stored_images: float32 [2, 4, 4, 40, 6, 128], P('gx', 'gy', 'gz'), as said below
- stored_curv: float32 [40], replicated, may hold values from 1 to 4
Outputs:
- multipliers: float32 [2, 4, 4, 6, 128, 128], P('gx', 'gy', 'gz')
- residual: float32 [2, 4, 4, 6, 128, 128], P('gx', 'gy', 'gz')
Inputs may be any that keep to these rules, and one draw needn't show every extreme that they name: `flexibility`: each subdomain's matrix is symmetric positive definite. `coarse_rows`: read as a [192, 192] matrix it is exactly symmetric: the inverse of G^T G for the coarse basis G of the present modes, with ones added on the diagonal of absent modes. `mode_counts`: modes numbered from the count on are absent. `block_map`: each subdomain's row names every interface position once. `stored_dirs`: both copies of every face agree: slot 2a of a subdomain equals slot 2a+1 of its lower neighbour along grid dimension a. `stored_images`: both copies of every face agree: slot 2a of a subdomain equals slot 2a+1 of its lower neighbour along grid dimension a.
All inputs are finite; a program needn't handle non-finite values.
Results may differ from a plain program's by a relative error of at most 0.0003.
Values sent between devices are 32-bit elements; how exact they have to be, the bound alone decides.
A program may use at most 128 MiB of HBM per device.

v0:
```python
import jax
import jax.numpy as jnp
from jax import lax
from jax.sharding import PartitionSpec as P

STORED = 40
ITERS = 3
precise = lax.Precision.HIGHEST
slot_signs = (-1.0, 1.0, -1.0, 1.0, -1.0, 1.0)


def extended(x, sides, width):
    for axis, dim in sides:
        peers, length = (lax.axis_size(axis), x.shape[dim])
        up = [(i, (i + 1) % peers) for i in range(peers)]
        down = [(j, i) for i, j in up]
        last = lax.slice_in_dim(x, length - width, length, axis=dim)
        initial = lax.slice_in_dim(x, 0, width, axis=dim)
        before = lax.ppermute(last, axis, up)
        after = lax.ppermute(initial, axis, down)
        x = jnp.concatenate([before, x, after], axis=dim)
    return x


def assemble(field):
    padded_x = extended(field[0:2], (("gx", 0),), 1)
    padded_y = extended(field[2:4], (("gy", 0),), 1)
    padded_z = extended(field[4:6], (("gz", 0),), 1)
    return jnp.stack(
        [
            field[0] + padded_x[0],
            field[1] + padded_x[3],
            field[2] + padded_y[0],
            field[3] + padded_y[3],
            field[4] + padded_z[0],
            field[5] + padded_z[3],
        ]
    )


def plus_inner(first, second):
    return jnp.sum(first[1::2] * second[1::2], axis=(0, 1))


def stored_inner(store, field):
    return jnp.einsum("isf,sfr->ir", store[:, 1::2], field[1::2], precision=precise)


def coarse_solve(loads, rows):
    return jnp.dot(
        rows, lax.all_gather(loads, ("gx", "gy", "gz"), axis=0, tiled=True), precision=precise
    )


def per_device(
    local_displacement,
    coarse_load,
    flexibility,
    block_map,
    mode_counts,
    mode_traces,
    coarse_rows,
    stored_dirs,
    stored_images,
    stored_curv,
):
    displacement = local_displacement[0, 0, 0]
    loads = coarse_load[0, 0, 0]
    flex = flexibility[0, 0, 0]
    mapping = block_map[0, 0, 0]
    rows = coarse_rows[0, 0, 0]
    dirs_store = stored_dirs[0, 0, 0]
    images_store = stored_images[0, 0, 0]
    signs = jnp.array(slot_signs, jnp.float32)
    field_signs = signs[:, None, None]
    nmodes = mode_traces.shape[3]
    present = (jnp.arange(nmodes, dtype=jnp.int32) < mode_counts[0, 0, 0]).astype(jnp.float32)
    signed = mode_traces[0, 0, 0] * present[:, None, None] * signs[None, :, None]
    size_nb = flex.shape[0]
    inverse = jnp.zeros((size_nb,), jnp.int32).at[mapping].set(jnp.arange(size_nb, dtype=jnp.int32))
    flex_face = jnp.take(jnp.take(flex, inverse, axis=0), inverse, axis=1)
    layout = displacement.shape

    def operate(field):
        flat = (field_signs * field).reshape(size_nb, layout[2])
        return jnp.dot(flex_face, flat, precision=precise).reshape(layout)

    def graph(alpha):
        return assemble(jnp.einsum("msf,mr->sfr", signed, alpha, precision=precise))

    def project(field):
        partial_loads = jnp.einsum("msf,sfr->mr", signed, field, precision=precise)
        return field - graph(coarse_solve(partial_loads, rows))

    lam = graph(coarse_solve(loads, rows))
    resid = project(assemble(field_signs * (displacement - operate(lam))))
    directions, images, curves = ([], [], [])
    for step in range(ITERS):
        local_rows = stored_inner(images_store, resid)
        if images:
            own_rows = jnp.stack([plus_inner(images[index], resid) for index in range(len(images))])
            local_rows = jnp.concatenate([local_rows, own_rows], axis=0)
        totals = lax.psum(local_rows, ("gx", "gy", "gz"))
        beta = totals[:STORED] / stored_curv[:, None]
        direction = resid - jnp.einsum("isf,ir->sfr", dirs_store, beta, precision=precise)
        for index in range(len(directions)):
            direction = direction - directions[index] * (totals[STORED + index] / curves[index])
        image_now = project(assemble(field_signs * operate(direction)))
        pair = lax.psum(
            jnp.stack([plus_inner(direction, image_now), plus_inner(direction, resid)]),
            ("gx", "gy", "gz"),
        )
        rate = pair[1] / pair[0]
        lam = lam + rate * direction
        resid = resid - rate * image_now
        directions.append(direction)
        images.append(image_now)
        curves.append(pair[0])
    return (lam[None, None, None], resid[None, None, None])


def solution(mesh):
    return jax.shard_map(
        per_device,
        mesh=mesh,
        in_specs=(
            P("gx", "gy", "gz", None, None, None),
            P("gx", "gy", "gz", None, None),
            P("gx", "gy", "gz", None, None),
            P("gx", "gy", "gz", None),
            P("gx", "gy", "gz"),
            P("gx", "gy", "gz", None, None, None),
            P("gx", "gy", "gz", None, None),
            P("gx", "gy", "gz", None, None, None),
            P("gx", "gy", "gz", None, None, None),
            P(),
        ),
        out_specs=(P("gx", "gy", "gz", None, None, None), P("gx", "gy", "gz", None, None, None)),
        check_vma=False,
    )
```

profile of v0, /device:TPU:10, one launch (start us, length us, event | category | flops | bytes accessed | tf_op | source)
XLA Modules:
  0.0 665.6 jit_solution(9631356648595068276)
XLA Ops:
  1.5 37.6 %all-gather = f32[1,1,1,192,128]{4,2,1,0,3:T(1,128)S(1)} all-gather(f32[1,1,1,6,128]{4,2,1,0,3:T(1,128)} %bitcast.275), channel_id=2, replica_groups=mesh['gx'=2,'gy'=4,'gz'=4] {'gx','gy','gz'}, dimensions={3}, use_global_device_ids=true | all-gather | bytes 101376 | tf_op jit(solution)/shard_map/all_gather | solution.py:51
  57.1 5.8 gather_fusion.1
  71.2 4.2 collective-permute-start.3
  78.9 3.7 fusion.4
  87.5 4.6 collective-permute-start.8
  99.1 37.6 %all-gather.1 = f32[32,6,128]{2,1,0:T(8,128)S(1)} all-gather(f32[1,6,128]{2,1,0:T(8,128)S(1)} %convolution_bitcast_fusion.14), channel_id=1, replica_groups=mesh['gx'=2,'gy'=4,'gz'=4] {'gx','gy','gz'}, dimensions={0}, use_global_device_ids=true | all-gather | bytes 101376 | tf_op jit(solution)/shard_map/all_gather | solution.py:51
  142.8 4.2 collective-permute-start.15
  153.1 43.5 %psum.42 = f32[40,128]{1,0:T(8,128)} all-reduce(f32[40,128]{1,0:T(8,128)S(1)} %convolution_bitcast_fusion.5), channel_id=1, replica_groups=mesh['gx'=2,'gy'=4,'gz'=4] {'gx','gy','gz'}, use_global_device_ids=true, to_apply=%region_1.2 | all-reduce | flops 5120 | bytes 40960 | tf_op jit(solution)/shard_map/psum | solution.py:103
  202.4 4.1 collective-permute-done.18
  214.1 39.5 %all-gather.2 = f32[32,6,128]{2,1,0:T(8,128)} all-gather(f32[1,6,128]{2,1,0:T(8,128)S(1)} %convolution_bitcast_fusion.13), channel_id=1, replica_groups=mesh['gx'=2,'gy'=4,'gz'=4] {'gx','gy','gz'}, dimensions={0}, use_global_device_ids=true | all-gather | bytes 101376 | tf_op jit(solution)/shard_map/all_gather | solution.py:51
  267.2 4.2 collective-permute-start.27
  278.5 42.5 %psum.43 = f32[2,128]{1,0:T(2,128)S(1)} all-reduce(f32[2,128]{1,0:T(2,128)S(1)} %pad_maximum_fusion.2), channel_id=1, replica_groups=mesh['gx'=2,'gy'=4,'gz'=4] {'gx','gy','gz'}, use_global_device_ids=true, to_apply=%region_4.5 | all-reduce | flops 256 | bytes 2048 | tf_op jit(solution)/shard_map/psum | solution.py:109
  324.6 39.2 %psum.44 = f32[41,128]{1,0:T(8,128)S(1)} all-reduce(f32[41,128]{1,0:T(8,128)S(1)} %pad_maximum_fusion), channel_id=1, replica_groups=mesh['gx'=2,'gy'=4,'gz'=4] {'gx','gy','gz'}, use_global_device_ids=true, to_apply=%region_6.7 | all-reduce | flops 5248 | bytes 41984 | tf_op jit(solution)/shard_map/psum | solution.py:103
  371.0 4.1 collective-permute-done.30
  378.5 3.9 collective-permute-done.31
  383.3 38.7 %all-gather.3 = f32[32,6,128]{2,1,0:T(8,128)S(1)} all-gather(f32[1,6,128]{2,1,0:T(8,128)S(1)} %convolution_bitcast_fusion.12), channel_id=1, replica_groups=mesh['gx'=2,'gy'=4,'gz'=4] {'gx','gy','gz'}, dimensions={0}, use_global_device_ids=true | all-gather | bytes 101376 | tf_op jit(solution)/shard_map/all_gather | solution.py:51
  433.3 4.2 collective-permute-start.39
  445.1 42.5 %psum.45 = f32[2,128]{1,0:T(2,128)} all-reduce(f32[2,128]{1,0:T(2,128)} %pad_maximum_fusion.3), channel_id=1, replica_groups=mesh['gx'=2,'gy'=4,'gz'=4] {'gx','gy','gz'}, use_global_device_ids=true, to_apply=%region_9.10 | all-reduce | flops 256 | bytes 2048 | tf_op jit(solution)/shard_map/psum | solution.py:109
  491.8 39.6 %psum.46 = f32[42,128]{1,0:T(8,128)S(1)} all-reduce(f32[42,128]{1,0:T(8,128)S(1)} %pad_maximum_fusion.1), channel_id=1, replica_groups=mesh['gx'=2,'gy'=4,'gz'=4] {'gx','gy','gz'}, use_global_device_ids=true, to_apply=%region_12.13 | all-reduce | flops 5376 | bytes 43008 | tf_op jit(solution)/shard_map/psum | solution.py:103
  534.9 3.7 convolution_multiply_fusion
  538.9 4.1 collective-permute-done.42
  550.9 38.9 %all-gather.4 = f32[32,6,128]{2,1,0:T(8,128)S(1)} all-gather(f32[1,6,128]{2,1,0:T(8,128)S(1)} %convolution_bitcast_fusion.11), channel_id=1, replica_groups=mesh['gx'=2,'gy'=4,'gz'=4] {'gx','gy','gz'}, dimensions={0}, use_global_device_ids=true | all-gather | bytes 101376 | tf_op jit(solution)/shard_map/all_gather | solution.py:51
  601.0 4.2 collective-permute-start.51
  611.6 42.5 %psum.47 = f32[2,128]{1,0:T(2,128)S(1)} all-reduce(f32[2,128]{1,0:T(2,128)S(1)} %pad_maximum_fusion.4), channel_id=1, replica_groups=mesh['gx'=2,'gy'=4,'gz'=4] {'gx','gy','gz'}, use_global_device_ids=true, to_apply=%region_15.16 | all-reduce | flops 256 | bytes 2048 | tf_op jit(solution)/shard_map/psum | solution.py:109
  (464 shorter events, 165.5 us)
Async XLA Ops:
  41.6 21.3 %collective-permute-start = (f32[1,128,128]{2,1,0:T(8,128)S(1)}, f32[1,128,128]{2,1,0:T(8,128)}, u32[]{:S(2)}, u32[]{:S(2)}) collective-permute-start(f32[1,128,128]{2,1,0:T(8,128)S(1)} %slice.456), channel_id=1, source_target_pairs={{0,16},{16,0},{1,17},{17,1},{2,18},{18,2},{3,19},{19,3},{4,20},{20... | collective-permute-start | bytes 196616 | tf_op jit(solution)/shard_map/ppermute | solution.py:19
  63.7 11.7 %collective-permute-start.1 = (f32[1,128,128]{2,1,0:T(8,128)S(1)}, f32[1,128,128]{2,1,0:T(8,128)}, u32[]{:S(2)}, u32[]{:S(2)}) collective-permute-start(f32[1,128,128]{2,1,0:T(8,128)S(1)} %get-tuple-element.63), channel_id=1, source_target_pairs={{16,0},{0,16},{17,1},{1,17},{18,2},{2,18},{19,3},{3,19},{20,4},{4,... | collective-permute-start | bytes 196616 | tf_op jit(solution)/shard_map/ppermute | solution.py:20
  87.0 11.1 %collective-permute-start.11 = (f32[1,128,128]{2,1,0:T(8,128)S(1)}, f32[1,128,128]{2,1,0:T(8,128)S(1)}, u32[]{:S(2)}, u32[]{:S(2)}) collective-permute-start(f32[1,128,128]{2,1,0:T(8,128)S(1)} %get-tuple-element.52), channel_id=1, source_target_pairs={{1,0},{2,1},{3,2},{0,3},{5,4},{6,5},{7,6},{4,7},{9,8},{10,9},{11,1... | collective-permute-start | bytes 196616 | tf_op jit(solution)/shard_map/ppermute | solution.py:20
  87.0 11.0 %collective-permute-start.10 = (f32[1,128,128]{2,1,0:T(8,128)S(1)}, f32[1,128,128]{2,1,0:T(8,128)S(1)}, u32[]{:S(2)}, u32[]{:S(2)}) collective-permute-start(f32[1,128,128]{2,1,0:T(8,128)S(1)} %get-tuple-element.54), channel_id=1, source_target_pairs={{0,1},{1,2},{2,3},{3,0},{4,5},{5,6},{6,7},{7,4},{8,9},{9,10},{10,1... | collective-permute-start | bytes 196616 | tf_op jit(solution)/shard_map/ppermute | solution.py:19
  87.5 8.9 %collective-permute-start.8 = (f32[1,128,128]{2,1,0:T(8,128)S(1)}, f32[1,128,128]{2,1,0:T(8,128)S(1)}, u32[]{:S(2)}, u32[]{:S(2)}) collective-permute-start(f32[1,128,128]{2,1,0:T(8,128)S(1)} %get-tuple-element.55), channel_id=1, source_target_pairs={{0,4},{4,8},{8,12},{12,0},{1,5},{5,9},{9,13},{13,1},{2,6},{6,10},{... | collective-permute-start | bytes 196616 | tf_op jit(solution)/shard_map/ppermute | solution.py:19
  142.2 9.3 %collective-permute-start.17 = (f32[1,128,128]{2,1,0:T(8,128)S(1)}, f32[1,128,128]{2,1,0:T(8,128)S(1)}, u32[]{:S(2)}, u32[]{:S(2)}) collective-permute-start(f32[1,128,128]{2,1,0:T(8,128)S(1)} %get-tuple-element.46), channel_id=1, source_target_pairs={{1,0},{2,1},{3,2},{0,3},{5,4},{6,5},{7,6},{4,7},{9,8},{10,9},{11,1... | collective-permute-start | bytes 196616 | tf_op jit(solution)/shard_map/ppermute | solution.py:20
  142.3 9.2 %collective-permute-start.16 = (f32[1,128,128]{2,1,0:T(8,128)S(1)}, f32[1,128,128]{2,1,0:T(8,128)S(1)}, u32[]{:S(2)}, u32[]{:S(2)}) collective-permute-start(f32[1,128,128]{2,1,0:T(8,128)S(1)} %get-tuple-element.48), channel_id=1, source_target_pairs={{0,1},{1,2},{2,3},{3,0},{4,5},{5,6},{6,7},{7,4},{8,9},{9,10},{10,1... | collective-permute-start | bytes 196616 | tf_op jit(solution)/shard_map/ppermute | solution.py:19
  142.8 8.6 %collective-permute-start.14 = (f32[1,128,128]{2,1,0:T(8,128)S(1)}, f32[1,128,128]{2,1,0:T(8,128)S(1)}, u32[]{:S(2)}, u32[]{:S(2)}) collective-permute-start(f32[1,128,128]{2,1,0:T(8,128)S(1)} %get-tuple-element.49), channel_id=1, source_target_pairs={{0,4},{4,8},{8,12},{12,0},{1,5},{5,9},{9,13},{13,1},{2,6},{6,10},{... | collective-permute-start | bytes 196616 | tf_op jit(solution)/shard_map/ppermute | solution.py:19
  142.8 8.7 %collective-permute-start.15 = (f32[1,128,128]{2,1,0:T(8,128)S(1)}, f32[1,128,128]{2,1,0:T(8,128)S(1)}, u32[]{:S(2)}, u32[]{:S(2)}) collective-permute-start(f32[1,128,128]{2,1,0:T(8,128)S(1)} %get-tuple-element.50), channel_id=1, source_target_pairs={{4,0},{8,4},{12,8},{0,12},{5,1},{9,5},{13,9},{1,13},{6,2},{10,6},{... | collective-permute-start | bytes 196616 | tf_op jit(solution)/shard_map/ppermute | solution.py:20
  257.8 8.7 %collective-permute-start.24 = (f32[1,128,128]{2,1,0:T(8,128)S(1)}, f32[1,128,128]{2,1,0:T(8,128)S(1)}, u32[]{:S(2)}, u32[]{:S(2)}) collective-permute-start(f32[1,128,128]{2,1,0:T(8,128)S(1)} %slice.480), channel_id=1, source_target_pairs={{0,16},{16,0},{1,17},{17,1},{2,18},{18,2},{3,19},{19,3},{4,20},{20... | collective-permute-start | bytes 196616 | tf_op jit(solution)/shard_map/ppermute | solution.py:19
  266.6 9.8 %collective-permute-start.29 = (f32[1,128,128]{2,1,0:T(8,128)S(1)}, f32[1,128,128]{2,1,0:T(8,128)S(1)}, u32[]{:S(2)}, u32[]{:S(2)}) collective-permute-start(f32[1,128,128]{2,1,0:T(8,128)S(1)} %get-tuple-element.34), channel_id=1, source_target_pairs={{1,0},{2,1},{3,2},{0,3},{5,4},{6,5},{7,6},{4,7},{9,8},{10,9},{11,1... | collective-permute-start | bytes 196616 | tf_op jit(solution)/shard_map/ppermute | solution.py:20
  266.7 9.7 %collective-permute-start.28 = (f32[1,128,128]{2,1,0:T(8,128)S(1)}, f32[1,128,128]{2,1,0:T(8,128)S(1)}, u32[]{:S(2)}, u32[]{:S(2)}) collective-permute-start(f32[1,128,128]{2,1,0:T(8,128)S(1)} %get-tuple-element.36), channel_id=1, source_target_pairs={{0,1},{1,2},{2,3},{3,0},{4,5},{5,6},{6,7},{7,4},{8,9},{9,10},{10,1... | collective-permute-start | bytes 196616 | tf_op jit(solution)/shard_map/ppermute | solution.py:19
  267.1 9.1 %collective-permute-start.26 = (f32[1,128,128]{2,1,0:T(8,128)S(1)}, f32[1,128,128]{2,1,0:T(8,128)S(1)}, u32[]{:S(2)}, u32[]{:S(2)}) collective-permute-start(f32[1,128,128]{2,1,0:T(8,128)S(1)} %get-tuple-element.37), channel_id=1, source_target_pairs={{0,4},{4,8},{8,12},{12,0},{1,5},{5,9},{9,13},{13,1},{2,6},{6,10},{... | collective-permute-start | bytes 196616 | tf_op jit(solution)/shard_map/ppermute | solution.py:19
  267.2 9.1 %collective-permute-start.27 = (f32[1,128,128]{2,1,0:T(8,128)S(1)}, f32[1,128,128]{2,1,0:T(8,128)S(1)}, u32[]{:S(2)}, u32[]{:S(2)}) collective-permute-start(f32[1,128,128]{2,1,0:T(8,128)S(1)} %get-tuple-element.38), channel_id=1, source_target_pairs={{4,0},{8,4},{12,8},{0,12},{5,1},{9,5},{13,9},{1,13},{6,2},{10,6},{... | collective-permute-start | bytes 196616 | tf_op jit(solution)/shard_map/ppermute | solution.py:20
  423.8 8.9 %collective-permute-start.36 = (f32[1,128,128]{2,1,0:T(8,128)S(1)}, f32[1,128,128]{2,1,0:T(8,128)S(1)}, u32[]{:S(2)}, u32[]{:S(2)}) collective-permute-start(f32[1,128,128]{2,1,0:T(8,128)S(1)} %slice.494), channel_id=1, source_target_pairs={{0,16},{16,0},{1,17},{17,1},{2,18},{18,2},{3,19},{19,3},{4,20},{20... | collective-permute-start | bytes 196616 | tf_op jit(solution)/shard_map/ppermute | solution.py:19
  432.7 9.8 %collective-permute-start.41 = (f32[1,128,128]{2,1,0:T(8,128)S(1)}, f32[1,128,128]{2,1,0:T(8,128)S(1)}, u32[]{:S(2)}, u32[]{:S(2)}) collective-permute-start(f32[1,128,128]{2,1,0:T(8,128)S(1)} %get-tuple-element.22), channel_id=1, source_target_pairs={{1,0},{2,1},{3,2},{0,3},{5,4},{6,5},{7,6},{4,7},{9,8},{10,9},{11,1... | collective-permute-start | bytes 196616 | tf_op jit(solution)/shard_map/ppermute | solution.py:20
  432.8 9.7 %collective-permute-start.40 = (f32[1,128,128]{2,1,0:T(8,128)S(1)}, f32[1,128,128]{2,1,0:T(8,128)S(1)}, u32[]{:S(2)}, u32[]{:S(2)}) collective-permute-start(f32[1,128,128]{2,1,0:T(8,128)S(1)} %get-tuple-element.24), channel_id=1, source_target_pairs={{0,1},{1,2},{2,3},{3,0},{4,5},{5,6},{6,7},{7,4},{8,9},{9,10},{10,1... | collective-permute-start | bytes 196616 | tf_op jit(solution)/shard_map/ppermute | solution.py:19
  433.3 9.1 %collective-permute-start.38 = (f32[1,128,128]{2,1,0:T(8,128)S(1)}, f32[1,128,128]{2,1,0:T(8,128)S(1)}, u32[]{:S(2)}, u32[]{:S(2)}) collective-permute-start(f32[1,128,128]{2,1,0:T(8,128)S(1)} %get-tuple-element.25), channel_id=1, source_target_pairs={{0,4},{4,8},{8,12},{12,0},{1,5},{5,9},{9,13},{13,1},{2,6},{6,10},{... | collective-permute-start | bytes 196616 | tf_op jit(solution)/shard_map/ppermute | solution.py:19
  433.3 9.1 %collective-permute-start.39 = (f32[1,128,128]{2,1,0:T(8,128)S(1)}, f32[1,128,128]{2,1,0:T(8,128)S(1)}, u32[]{:S(2)}, u32[]{:S(2)}) collective-permute-start(f32[1,128,128]{2,1,0:T(8,128)S(1)} %get-tuple-element.26), channel_id=1, source_target_pairs={{4,0},{8,4},{12,8},{0,12},{5,1},{9,5},{13,9},{1,13},{6,2},{10,6},{... | collective-permute-start | bytes 196616 | tf_op jit(solution)/shard_map/ppermute | solution.py:20
  591.7 8.7 %collective-permute-start.48 = (f32[1,128,128]{2,1,0:T(8,128)S(1)}, f32[1,128,128]{2,1,0:T(8,128)S(1)}, u32[]{:S(2)}, u32[]{:S(2)}) collective-permute-start(f32[1,128,128]{2,1,0:T(8,128)S(1)} %slice.509), channel_id=1, source_target_pairs={{0,16},{16,0},{1,17},{17,1},{2,18},{18,2},{3,19},{19,3},{4,20},{20... | collective-permute-start | bytes 196616 | tf_op jit(solution)/shard_map/ppermute | solution.py:19
  600.4 9.8 %collective-permute-start.53 = (f32[1,128,128]{2,1,0:T(8,128)S(1)}, f32[1,128,128]{2,1,0:T(8,128)S(1)}, u32[]{:S(2)}, u32[]{:S(2)}) collective-permute-start(f32[1,128,128]{2,1,0:T(8,128)S(1)} %get-tuple-element.10), channel_id=1, source_target_pairs={{1,0},{2,1},{3,2},{0,3},{5,4},{6,5},{7,6},{4,7},{9,8},{10,9},{11,1... | collective-permute-start | bytes 196616 | tf_op jit(solution)/shard_map/ppermute | solution.py:20
  600.5 9.7 %collective-permute-start.52 = (f32[1,128,128]{2,1,0:T(8,128)S(1)}, f32[1,128,128]{2,1,0:T(8,128)S(1)}, u32[]{:S(2)}, u32[]{:S(2)}) collective-permute-start(f32[1,128,128]{2,1,0:T(8,128)S(1)} %get-tuple-element.12), channel_id=1, source_target_pairs={{0,1},{1,2},{2,3},{3,0},{4,5},{5,6},{6,7},{7,4},{8,9},{9,10},{10,1... | collective-permute-start | bytes 196616 | tf_op jit(solution)/shard_map/ppermute | solution.py:19
  601.0 9.1 %collective-permute-start.50 = (f32[1,128,128]{2,1,0:T(8,128)S(1)}, f32[1,128,128]{2,1,0:T(8,128)S(1)}, u32[]{:S(2)}, u32[]{:S(2)}) collective-permute-start(f32[1,128,128]{2,1,0:T(8,128)S(1)} %get-tuple-element.13), channel_id=1, source_target_pairs={{0,4},{4,8},{8,12},{12,0},{1,5},{5,9},{9,13},{13,1},{2,6},{6,10},{... | collective-permute-start | bytes 196616 | tf_op jit(solution)/shard_map/ppermute | solution.py:19
  601.0 9.1 %collective-permute-start.51 = (f32[1,128,128]{2,1,0:T(8,128)S(1)}, f32[1,128,128]{2,1,0:T(8,128)S(1)}, u32[]{:S(2)}, u32[]{:S(2)}) collective-permute-start(f32[1,128,128]{2,1,0:T(8,128)S(1)} %get-tuple-element.14), channel_id=1, source_target_pairs={{4,0},{8,4},{12,8},{0,12},{5,1},{9,5},{13,9},{1,13},{6,2},{10,6},{... | collective-permute-start | bytes 196616 | tf_op jit(solution)/shard_map/ppermute | solution.py:20
  (126 other events, 1106.9 us)
where the time goes:
time: 668 us; the launch traced here: 666 us
  blocking collectives  442 us (66%)
  other arithmetic  60.4 us (9%)
  starting transfers between devices  49.7 us (7%)
  waiting for transfers between devices  45.8 us (7%)
  matrix products  34.5 us (5%)
  local copies, waits for them, and re-layouts  29.8 us (4%)
    all_gather x5, blocking collectives, coarse_solve(): lax.all_gather(loads, ('gx', 'gy', 'gz'), axis=0, tiled=True)  192 us
    psum x3, blocking collectives, per_device(): lax.psum(jnp.stack([plus_inner(direction, image_now), plus_inner(directio...  127 us
    psum x3, blocking collectives, per_device(): totals = lax.psum(local_rows, ('gx', 'gy', 'gz'))  122 us
    unnamed x76, other arithmetic  32.8 us
    ppermute x27, starting transfers between devices, extended(): after = lax.ppermute(initial, axis, down)  29.9 us
    ppermute x27, waiting for transfers between devices, extended(): after = lax.ppermute(initial, axis, down)  28.2 us
    ppermute x27, starting transfers between devices, extended(): before = lax.ppermute(last, axis, up)  19.8 us
    ppermute x27, waiting for transfers between devices, extended(): before = lax.ppermute(last, axis, up)  17.5 us
  transfers between devices with their start and end apart: 54, of which 15 were waited for; matrix products, arithmetic and copies ran while one was open for 9% of the time, Pallas kernels for 0%

commit v1 on v0

--- a/solution.py
+++ b/solution.py
@@ -100,7 +100,9 @@
         if images:
             own_rows = jnp.stack([plus_inner(images[index], resid) for index in range(len(images))])
             local_rows = jnp.concatenate([local_rows, own_rows], axis=0)
-        totals = lax.psum(local_rows, ("gx", "gy", "gz"))
+        totals = local_rows
+        for dev_j in ("gx", ("gy", "gz")):
+            totals = lax.psum(totals, dev_j)
         beta = totals[:STORED] / stored_curv[:, None]
         direction = resid - jnp.einsum("isf,ir->sfr", dirs_store, beta, precision=precise)
         for index in range(len(directions)):

time: 668 us -> 737 us (1.10)
  blocking collectives: 442 us -> 489 us
  starting transfers between devices: 49.7 us -> 82.2 us
  waiting for transfers between devices: 45.8 us -> 31.7 us
    psum x3 -> x6, blocking collectives: 122 us -> 172 us  [per_device(): totals = lax.psum(totals, dev_j)]
    ppermute x27, starting transfers between devices: 29.9 us -> 60.9 us  [extended(): after = lax.ppermute(initial, axis, down)]
    ppermute x27, waiting for transfers between devices: 17.5 us -> 9.65 us  [extended(): before = lax.ppermute(last, axis, up)]
  transfers between devices with their start and end apart: 54 -> 54, of which waited for: 15 -> 14; matrix products, arithmetic and copies ran while one was open for 9% -> 8% of each run, Pallas kernels for 0% -> 0%
where the time goes in v1:
time: 737 us; the launch traced here: 735 us
  blocking collectives  489 us (66%)
  starting transfers between devices  82.2 us (11%)
  other arithmetic  64.4 us (9%)
  matrix products  34.5 us (5%)
  waiting for transfers between devices  31.7 us (4%)
  local copies, waits for them, and re-layouts  29.9 us (4%)
    all_gather x5, blocking collectives, coarse_solve(): lax.all_gather(loads, ('gx', 'gy', 'gz'), axis=0, tiled=True)  187 us
    psum x6, blocking collectives, per_device(): totals = lax.psum(totals, dev_j)  172 us
    psum x3, blocking collectives, per_device(): lax.psum(jnp.stack([plus_inner(direction, image_now), plus_inner(directio...  129 us
    ppermute x27, starting transfers between devices, extended(): after = lax.ppermute(initial, axis, down)  60.9 us
    unnamed x76, other arithmetic  36.1 us
    ppermute x27, waiting for transfers between devices, extended(): after = lax.ppermute(initial, axis, down)  22 us
    ppermute x27, starting transfers between devices, extended(): before = lax.ppermute(last, axis, up)  21.2 us
    dot_general x4, matrix products, operate(): return jnp.dot(flex_face, flat, precision=precise).reshape(layout)  14.8 us
  transfers between devices with their start and end apart: 54, of which 14 were waited for; matrix products, arithmetic and copies ran while one was open for 8% of the time, Pallas kernels for 0%

profile of v1, /device:TPU:10, one launch (start us, length us, event | category | flops | bytes accessed | tf_op | source)
XLA Modules:
  0.0 734.7 jit_solution(1976140282468337180)
XLA Ops:
  1.5 37.6 %all-gather = f32[1,1,1,192,128]{4,2,1,0,3:T(1,128)S(1)} all-gather(f32[1,1,1,6,128]{4,2,1,0,3:T(1,128)} %bitcast.275), channel_id=2, replica_groups=mesh['gx'=2,'gy'=4,'gz'=4] {'gx','gy','gz'}, dimensions={3}, use_global_device_ids=true | all-gather | bytes 101376 | tf_op jit(solution)/shard_map/all_gather | solution.py:51
  57.1 5.7 gather_fusion.1
  71.2 4.2 collective-permute-start.3
  87.5 4.6 collective-permute-start.8
  99.1 37.6 %all-gather.1 = f32[32,6,128]{2,1,0:T(8,128)S(1)} all-gather(f32[1,6,128]{2,1,0:T(8,128)S(1)} %convolution_bitcast_fusion.14), channel_id=1, replica_groups=mesh['gx'=2,'gy'=4,'gz'=4] {'gx','gy','gz'}, dimensions={0}, use_global_device_ids=true | all-gather | bytes 101376 | tf_op jit(solution)/shard_map/all_gather | solution.py:51
  142.7 4.2 collective-permute-start.15
  153.0 8.1 %psum.63 = f32[40,128]{1,0:T(8,128)S(1)} all-reduce(f32[40,128]{1,0:T(8,128)S(1)} %convolution_bitcast_fusion.5), channel_id=1, replica_groups=mesh['gx'=2,'gy'=4,'gz'=4] {'gx'}, use_global_device_ids=true, to_apply=%region_1.2 | all-reduce | flops 5120 | bytes 40960 | tf_op jit(solution)/shard_map/psum | solution.py:105
  161.1 53.1 %psum.64 = f32[40,128]{1,0:T(8,128)} all-reduce(f32[40,128]{1,0:T(8,128)S(1)} %psum.63), channel_id=1, replica_groups=mesh['gx'=2,'gy'=4,'gz'=4] {'gy','gz'}, use_global_device_ids=true, to_apply=%region_2.3 | all-reduce | flops 5120 | bytes 40960 | tf_op jit(solution)/shard_map/psum | solution.py:105
  225.0 8.4 %collective-permute-start.21 = (f32[1,128,128]{2,1,0:T(8,128)S(1)}, f32[1,128,128]{2,1,0:T(8,128)S(1)}, u32[]{:S(2)}, u32[]{:S(2)}) collective-permute-start(f32[1,128,128]{2,1,0:T(8,128)S(1)} %get-tuple-element.44), channel_id=1, source_target_pairs={{4,0},{8,4},{12,8},{0,12},{5,1},{9,5},{13,9},{1,13},{6,2},{10,6},{... | collective-permute-start | bytes 196616 | tf_op jit(solution)/shard_map/ppermute | solution.py:20
  238.5 39.0 %all-gather.2 = f32[32,6,128]{2,1,0:T(8,128)} all-gather(f32[1,6,128]{2,1,0:T(8,128)S(1)} %convolution_bitcast_fusion.13), channel_id=1, replica_groups=mesh['gx'=2,'gy'=4,'gz'=4] {'gx','gy','gz'}, dimensions={0}, use_global_device_ids=true | all-gather | bytes 101376 | tf_op jit(solution)/shard_map/all_gather | solution.py:51
  292.5 4.2 collective-permute-start.27
  303.1 43.1 %psum.65 = f32[2,128]{1,0:T(2,128)S(1)} all-reduce(f32[2,128]{1,0:T(2,128)S(1)} %pad_maximum_fusion.2), channel_id=1, replica_groups=mesh['gx'=2,'gy'=4,'gz'=4] {'gx','gy','gz'}, use_global_device_ids=true, to_apply=%region_5.6 | all-reduce | flops 256 | bytes 2048 | tf_op jit(solution)/shard_map/psum | solution.py:111
  350.0 6.9 psum.66
  356.8 48.8 %psum.67 = f32[41,128]{1,0:T(8,128)S(1)} all-reduce(f32[41,128]{1,0:T(8,128)S(1)} %psum.66), channel_id=1, replica_groups=mesh['gx'=2,'gy'=4,'gz'=4] {'gy','gz'}, use_global_device_ids=true, to_apply=%region_8.9 | all-reduce | flops 5248 | bytes 41984 | tf_op jit(solution)/shard_map/psum | solution.py:105
  417.5 8.5 %collective-permute-start.33 = (f32[1,128,128]{2,1,0:T(8,128)S(1)}, f32[1,128,128]{2,1,0:T(8,128)S(1)}, u32[]{:S(2)}, u32[]{:S(2)}) collective-permute-start(f32[1,128,128]{2,1,0:T(8,128)S(1)} %get-tuple-element.32), channel_id=1, source_target_pairs={{4,0},{8,4},{12,8},{0,12},{5,1},{9,5},{13,9},{1,13},{6,2},{10,6},{... | collective-permute-start | bytes 196616 | tf_op jit(solution)/shard_map/ppermute | solution.py:20
  431.2 36.4 %all-gather.3 = f32[32,6,128]{2,1,0:T(8,128)S(1)} all-gather(f32[1,6,128]{2,1,0:T(8,128)S(1)} %convolution_bitcast_fusion.12), channel_id=1, replica_groups=mesh['gx'=2,'gy'=4,'gz'=4] {'gx','gy','gz'}, dimensions={0}, use_global_device_ids=true | all-gather | bytes 101376 | tf_op jit(solution)/shard_map/all_gather | solution.py:51
  480.5 4.2 collective-permute-start.39
  491.7 43.3 %psum.68 = f32[2,128]{1,0:T(2,128)} all-reduce(f32[2,128]{1,0:T(2,128)} %pad_maximum_fusion.3), channel_id=1, replica_groups=mesh['gx'=2,'gy'=4,'gz'=4] {'gx','gy','gz'}, use_global_device_ids=true, to_apply=%region_11.12 | all-reduce | flops 256 | bytes 2048 | tf_op jit(solution)/shard_map/psum | solution.py:111
  539.2 6.8 psum.69
  546.0 48.7 %psum.70 = f32[42,128]{1,0:T(8,128)S(1)} all-reduce(f32[42,128]{1,0:T(8,128)S(1)} %psum.69), channel_id=1, replica_groups=mesh['gx'=2,'gy'=4,'gz'=4] {'gy','gz'}, use_global_device_ids=true, to_apply=%region_15.16 | all-reduce | flops 5376 | bytes 43008 | tf_op jit(solution)/shard_map/psum | solution.py:105
  606.9 8.4 %collective-permute-start.45 = (f32[1,128,128]{2,1,0:T(8,128)S(1)}, f32[1,128,128]{2,1,0:T(8,128)S(1)}, u32[]{:S(2)}, u32[]{:S(2)}) collective-permute-start(f32[1,128,128]{2,1,0:T(8,128)S(1)} %get-tuple-element.20), channel_id=1, source_target_pairs={{4,0},{8,4},{12,8},{0,12},{5,1},{9,5},{13,9},{1,13},{6,2},{10,6},{... | collective-permute-start | bytes 196616 | tf_op jit(solution)/shard_map/ppermute | solution.py:20
  620.6 36.5 %all-gather.4 = f32[32,6,128]{2,1,0:T(8,128)S(1)} all-gather(f32[1,6,128]{2,1,0:T(8,128)S(1)} %convolution_bitcast_fusion.11), channel_id=1, replica_groups=mesh['gx'=2,'gy'=4,'gz'=4] {'gx','gy','gz'}, dimensions={0}, use_global_device_ids=true | all-gather | bytes 101376 | tf_op jit(solution)/shard_map/all_gather | solution.py:51
  670.1 4.2 collective-permute-start.51
  680.1 43.1 %psum.71 = f32[2,128]{1,0:T(2,128)S(1)} all-reduce(f32[2,128]{1,0:T(2,128)S(1)} %pad_maximum_fusion.4), channel_id=1, replica_groups=mesh['gx'=2,'gy'=4,'gz'=4] {'gx','gy','gz'}, use_global_device_ids=true, to_apply=%region_18.19 | all-reduce | flops 256 | bytes 2048 | tf_op jit(solution)/shard_map/psum | solution.py:111
  (461 shorter events, 186.2 us)
Async XLA Ops:
  41.6 21.3 %collective-permute-start = (f32[1,128,128]{2,1,0:T(8,128)S(1)}, f32[1,128,128]{2,1,0:T(8,128)}, u32[]{:S(2)}, u32[]{:S(2)}) collective-permute-start(f32[1,128,128]{2,1,0:T(8,128)S(1)} %slice.456), channel_id=1, source_target_pairs={{0,16},{16,0},{1,17},{17,1},{2,18},{18,2},{3,19},{19,3},{4,20},{20... | collective-permute-start | bytes 196616 | tf_op jit(solution)/shard_map/ppermute | solution.py:19
  63.7 11.6 %collective-permute-start.1 = (f32[1,128,128]{2,1,0:T(8,128)S(1)}, f32[1,128,128]{2,1,0:T(8,128)}, u32[]{:S(2)}, u32[]{:S(2)}) collective-permute-start(f32[1,128,128]{2,1,0:T(8,128)S(1)} %get-tuple-element.63), channel_id=1, source_target_pairs={{16,0},{0,16},{17,1},{1,17},{18,2},{2,18},{19,3},{3,19},{20,4},{4,... | collective-permute-start | bytes 196616 | tf_op jit(solution)/shard_map/ppermute | solution.py:20
  86.9 11.1 %collective-permute-start.11 = (f32[1,128,128]{2,1,0:T(8,128)S(1)}, f32[1,128,128]{2,1,0:T(8,128)S(1)}, u32[]{:S(2)}, u32[]{:S(2)}) collective-permute-start(f32[1,128,128]{2,1,0:T(8,128)S(1)} %get-tuple-element.52), channel_id=1, source_target_pairs={{1,0},{2,1},{3,2},{0,3},{5,4},{6,5},{7,6},{4,7},{9,8},{10,9},{11,1... | collective-permute-start | bytes 196616 | tf_op jit(solution)/shard_map/ppermute | solution.py:20
  87.0 11.0 %collective-permute-start.10 = (f32[1,128,128]{2,1,0:T(8,128)S(1)}, f32[1,128,128]{2,1,0:T(8,128)S(1)}, u32[]{:S(2)}, u32[]{:S(2)}) collective-permute-start(f32[1,128,128]{2,1,0:T(8,128)S(1)} %get-tuple-element.54), channel_id=1, source_target_pairs={{0,1},{1,2},{2,3},{3,0},{4,5},{5,6},{6,7},{7,4},{8,9},{9,10},{10,1... | collective-permute-start | bytes 196616 | tf_op jit(solution)/shard_map/ppermute | solution.py:19
  142.2 9.3 %collective-permute-start.17 = (f32[1,128,128]{2,1,0:T(8,128)S(1)}, f32[1,128,128]{2,1,0:T(8,128)S(1)}, u32[]{:S(2)}, u32[]{:S(2)}) collective-permute-start(f32[1,128,128]{2,1,0:T(8,128)S(1)} %get-tuple-element.46), channel_id=1, source_target_pairs={{1,0},{2,1},{3,2},{0,3},{5,4},{6,5},{7,6},{4,7},{9,8},{10,9},{11,1... | collective-permute-start | bytes 196616 | tf_op jit(solution)/shard_map/ppermute | solution.py:20
  142.2 9.2 %collective-permute-start.16 = (f32[1,128,128]{2,1,0:T(8,128)S(1)}, f32[1,128,128]{2,1,0:T(8,128)S(1)}, u32[]{:S(2)}, u32[]{:S(2)}) collective-permute-start(f32[1,128,128]{2,1,0:T(8,128)S(1)} %get-tuple-element.48), channel_id=1, source_target_pairs={{0,1},{1,2},{2,3},{3,0},{4,5},{5,6},{6,7},{7,4},{8,9},{9,10},{10,1... | collective-permute-start | bytes 196616 | tf_op jit(solution)/shard_map/ppermute | solution.py:19
  224.5 13.4 %collective-permute-start.23 = (f32[1,128,128]{2,1,0:T(8,128)S(1)}, f32[1,128,128]{2,1,0:T(8,128)S(1)}, u32[]{:S(2)}, u32[]{:S(2)}) collective-permute-start(f32[1,128,128]{2,1,0:T(8,128)S(1)} %get-tuple-element.40), channel_id=1, source_target_pairs={{1,0},{2,1},{3,2},{0,3},{5,4},{6,5},{7,6},{4,7},{9,8},{10,9},{11,1... | collective-permute-start | bytes 196616 | tf_op jit(solution)/shard_map/ppermute | solution.py:20
  224.5 13.3 %collective-permute-start.22 = (f32[1,128,128]{2,1,0:T(8,128)S(1)}, f32[1,128,128]{2,1,0:T(8,128)S(1)}, u32[]{:S(2)}, u32[]{:S(2)}) collective-permute-start(f32[1,128,128]{2,1,0:T(8,128)S(1)} %get-tuple-element.42), channel_id=1, source_target_pairs={{0,1},{1,2},{2,3},{3,0},{4,5},{5,6},{6,7},{7,4},{8,9},{9,10},{10,1... | collective-permute-start | bytes 196616 | tf_op jit(solution)/shard_map/ppermute | solution.py:19
  225.0 12.7 %collective-permute-start.20 = (f32[1,128,128]{2,1,0:T(8,128)S(1)}, f32[1,128,128]{2,1,0:T(8,128)S(1)}, u32[]{:S(2)}, u32[]{:S(2)}) collective-permute-start(f32[1,128,128]{2,1,0:T(8,128)S(1)} %get-tuple-element.43), channel_id=1, source_target_pairs={{0,4},{4,8},{8,12},{12,0},{1,5},{5,9},{9,13},{13,1},{2,6},{6,10},{... | collective-permute-start | bytes 196616 | tf_op jit(solution)/shard_map/ppermute | solution.py:19
  225.0 12.8 %collective-permute-start.21 = (f32[1,128,128]{2,1,0:T(8,128)S(1)}, f32[1,128,128]{2,1,0:T(8,128)S(1)}, u32[]{:S(2)}, u32[]{:S(2)}) collective-permute-start(f32[1,128,128]{2,1,0:T(8,128)S(1)} %get-tuple-element.44), channel_id=1, source_target_pairs={{4,0},{8,4},{12,8},{0,12},{5,1},{9,5},{13,9},{1,13},{6,2},{10,6},{... | collective-permute-start | bytes 196616 | tf_op jit(solution)/shard_map/ppermute | solution.py:20
  281.7 9.0 %collective-permute-start.24 = (f32[1,128,128]{2,1,0:T(8,128)S(1)}, f32[1,128,128]{2,1,0:T(8,128)S(1)}, u32[]{:S(2)}, u32[]{:S(2)}) collective-permute-start(f32[1,128,128]{2,1,0:T(8,128)S(1)} %slice.480), channel_id=1, source_target_pairs={{0,16},{16,0},{1,17},{17,1},{2,18},{18,2},{3,19},{19,3},{4,20},{20... | collective-permute-start | bytes 196616 | tf_op jit(solution)/shard_map/ppermute | solution.py:19
  290.7 10.3 %collective-permute-start.29 = (f32[1,128,128]{2,1,0:T(8,128)S(1)}, f32[1,128,128]{2,1,0:T(8,128)S(1)}, u32[]{:S(2)}, u32[]{:S(2)}) collective-permute-start(f32[1,128,128]{2,1,0:T(8,128)S(1)} %get-tuple-element.34), channel_id=1, source_target_pairs={{1,0},{2,1},{3,2},{0,3},{5,4},{6,5},{7,6},{4,7},{9,8},{10,9},{11,1... | collective-permute-start | bytes 196616 | tf_op jit(solution)/shard_map/ppermute | solution.py:20
  417.0 13.4 %collective-permute-start.35 = (f32[1,128,128]{2,1,0:T(8,128)S(1)}, f32[1,128,128]{2,1,0:T(8,128)S(1)}, u32[]{:S(2)}, u32[]{:S(2)}) collective-permute-start(f32[1,128,128]{2,1,0:T(8,128)S(1)} %get-tuple-element.28), channel_id=1, source_target_pairs={{1,0},{2,1},{3,2},{0,3},{5,4},{6,5},{7,6},{4,7},{9,8},{10,9},{11,1... | collective-permute-start | bytes 196616 | tf_op jit(solution)/shard_map/ppermute | solution.py:20
  417.0 13.3 %collective-permute-start.34 = (f32[1,128,128]{2,1,0:T(8,128)S(1)}, f32[1,128,128]{2,1,0:T(8,128)S(1)}, u32[]{:S(2)}, u32[]{:S(2)}) collective-permute-start(f32[1,128,128]{2,1,0:T(8,128)S(1)} %get-tuple-element.30), channel_id=1, source_target_pairs={{0,1},{1,2},{2,3},{3,0},{4,5},{5,6},{6,7},{7,4},{8,9},{9,10},{10,1... | collective-permute-start | bytes 196616 | tf_op jit(solution)/shard_map/ppermute | solution.py:19
  417.5 12.7 %collective-permute-start.32 = (f32[1,128,128]{2,1,0:T(8,128)S(1)}, f32[1,128,128]{2,1,0:T(8,128)S(1)}, u32[]{:S(2)}, u32[]{:S(2)}) collective-permute-start(f32[1,128,128]{2,1,0:T(8,128)S(1)} %get-tuple-element.31), channel_id=1, source_target_pairs={{0,4},{4,8},{8,12},{12,0},{1,5},{5,9},{9,13},{13,1},{2,6},{6,10},{... | collective-permute-start | bytes 196616 | tf_op jit(solution)/shard_map/ppermute | solution.py:19
  417.5 12.8 %collective-permute-start.33 = (f32[1,128,128]{2,1,0:T(8,128)S(1)}, f32[1,128,128]{2,1,0:T(8,128)S(1)}, u32[]{:S(2)}, u32[]{:S(2)}) collective-permute-start(f32[1,128,128]{2,1,0:T(8,128)S(1)} %get-tuple-element.32), channel_id=1, source_target_pairs={{4,0},{8,4},{12,8},{0,12},{5,1},{9,5},{13,9},{1,13},{6,2},{10,6},{... | collective-permute-start | bytes 196616 | tf_op jit(solution)/shard_map/ppermute | solution.py:20
  469.4 9.4 %collective-permute-start.36 = (f32[1,128,128]{2,1,0:T(8,128)S(1)}, f32[1,128,128]{2,1,0:T(8,128)S(1)}, u32[]{:S(2)}, u32[]{:S(2)}) collective-permute-start(f32[1,128,128]{2,1,0:T(8,128)S(1)} %slice.494), channel_id=1, source_target_pairs={{0,16},{16,0},{1,17},{17,1},{2,18},{18,2},{3,19},{19,3},{4,20},{20... | collective-permute-start | bytes 196616 | tf_op jit(solution)/shard_map/ppermute | solution.py:19
  478.9 10.2 %collective-permute-start.41 = (f32[1,128,128]{2,1,0:T(8,128)S(1)}, f32[1,128,128]{2,1,0:T(8,128)S(1)}, u32[]{:S(2)}, u32[]{:S(2)}) collective-permute-start(f32[1,128,128]{2,1,0:T(8,128)S(1)} %get-tuple-element.22), channel_id=1, source_target_pairs={{1,0},{2,1},{3,2},{0,3},{5,4},{6,5},{7,6},{4,7},{9,8},{10,9},{11,1... | collective-permute-start | bytes 196616 | tf_op jit(solution)/shard_map/ppermute | solution.py:20
  606.4 13.4 %collective-permute-start.47 = (f32[1,128,128]{2,1,0:T(8,128)S(1)}, f32[1,128,128]{2,1,0:T(8,128)S(1)}, u32[]{:S(2)}, u32[]{:S(2)}) collective-permute-start(f32[1,128,128]{2,1,0:T(8,128)S(1)} %get-tuple-element.16), channel_id=1, source_target_pairs={{1,0},{2,1},{3,2},{0,3},{5,4},{6,5},{7,6},{4,7},{9,8},{10,9},{11,1... | collective-permute-start | bytes 196616 | tf_op jit(solution)/shard_map/ppermute | solution.py:20
  606.4 13.3 %collective-permute-start.46 = (f32[1,128,128]{2,1,0:T(8,128)S(1)}, f32[1,128,128]{2,1,0:T(8,128)S(1)}, u32[]{:S(2)}, u32[]{:S(2)}) collective-permute-start(f32[1,128,128]{2,1,0:T(8,128)S(1)} %get-tuple-element.18), channel_id=1, source_target_pairs={{0,1},{1,2},{2,3},{3,0},{4,5},{5,6},{6,7},{7,4},{8,9},{9,10},{10,1... | collective-permute-start | bytes 196616 | tf_op jit(solution)/shard_map/ppermute | solution.py:19
  606.9 12.7 %collective-permute-start.44 = (f32[1,128,128]{2,1,0:T(8,128)S(1)}, f32[1,128,128]{2,1,0:T(8,128)S(1)}, u32[]{:S(2)}, u32[]{:S(2)}) collective-permute-start(f32[1,128,128]{2,1,0:T(8,128)S(1)} %get-tuple-element.19), channel_id=1, source_target_pairs={{0,4},{4,8},{8,12},{12,0},{1,5},{5,9},{9,13},{13,1},{2,6},{6,10},{... | collective-permute-start | bytes 196616 | tf_op jit(solution)/shard_map/ppermute | solution.py:19
  606.9 12.8 %collective-permute-start.45 = (f32[1,128,128]{2,1,0:T(8,128)S(1)}, f32[1,128,128]{2,1,0:T(8,128)S(1)}, u32[]{:S(2)}, u32[]{:S(2)}) collective-permute-start(f32[1,128,128]{2,1,0:T(8,128)S(1)} %get-tuple-element.20), channel_id=1, source_target_pairs={{4,0},{8,4},{12,8},{0,12},{5,1},{9,5},{13,9},{1,13},{6,2},{10,6},{... | collective-permute-start | bytes 196616 | tf_op jit(solution)/shard_map/ppermute | solution.py:20
  659.0 9.4 %collective-permute-start.48 = (f32[1,128,128]{2,1,0:T(8,128)S(1)}, f32[1,128,128]{2,1,0:T(8,128)S(1)}, u32[]{:S(2)}, u32[]{:S(2)}) collective-permute-start(f32[1,128,128]{2,1,0:T(8,128)S(1)} %slice.509), channel_id=1, source_target_pairs={{0,16},{16,0},{1,17},{17,1},{2,18},{18,2},{3,19},{19,3},{4,20},{20... | collective-permute-start | bytes 196616 | tf_op jit(solution)/shard_map/ppermute | solution.py:19
  668.4 10.3 %collective-permute-start.53 = (f32[1,128,128]{2,1,0:T(8,128)S(1)}, f32[1,128,128]{2,1,0:T(8,128)S(1)}, u32[]{:S(2)}, u32[]{:S(2)}) collective-permute-start(f32[1,128,128]{2,1,0:T(8,128)S(1)} %get-tuple-element.10), channel_id=1, source_target_pairs={{1,0},{2,1},{3,2},{0,3},{5,4},{6,5},{7,6},{4,7},{9,8},{10,9},{11,1... | collective-permute-start | bytes 196616 | tf_op jit(solution)/shard_map/ppermute | solution.py:20
  (123 other events, 1219.5 us)
